TPU v7x, 128 devices: a whole 4x4x4 slice. The times are simulated.
128 devices in a mesh: px: 16 (over y, x), py: 8 (over z, core).
Axes of the slice: x: 4, y: 4, z: 4, core: 2. Of those that a mesh axis runs over, the one named last changes fastest.
Arguments:
- node_latents: bfloat16 [256, 160, 512], P('px', 'py'), may hold values from -6 to 6
- fine_edges: bfloat16 [256, 160, 6, 512], P('px', 'py'), may hold values from -6 to 6
- long_edges: bfloat16 [20480, 512], P(('px', 'py')), may hold values from -6 to 6
- neighbours: int32 [256, 160, 6], P('px', 'py'), may hold values from 0 to 7, as said below
- coarse_slots: int32 [2560], P(('px', 'py')), may hold values from 0 to 319, as said below
- long_senders: int32 [20480], P(('px', 'py')), may hold values from 0 to 2559
- long_receivers: int32 [20480], P(('px', 'py')), may hold values from 0 to 2559, as said below
- edge_inner: bfloat16 [2, 1536, 512], replicated, may hold values from -0.15625 to 0.15625
- edge_outer: bfloat16 [2, 512, 512], replicated, may hold values from -0.25 to 0.25
- edge_gain: float32 [2, 512], replicated, may hold values from 0.5 to 1.5
- node_inner: bfloat16 [2, 1024, 512], replicated, may hold values from -0.1875 to 0.1875
- node_outer: bfloat16 [2, 512, 512], replicated, may hold values from -0.25 to 0.25
- node_gain: float32 [2, 512], replicated, may hold values from 0.5 to 1.5
Outputs:
- new_nodes: bfloat16 [256, 160, 512], P('px', 'py')
- new_fine: bfloat16 [256, 160, 6, 512], P('px', 'py')
- new_long: bfloat16 [20480, 512], P(('px', 'py'))
Inputs may be any that keep to these rules, and one draw needn't show every extreme that they name: `neighbours`: the 6 codes of one node are different. `coarse_slots`: the 20 entries of one device's block are different. `long_receivers`: among the 160 long edges of one device, at most 3 have receivers c with the same c // 20, and on every device some such group has exactly 3.
All inputs are finite; a program needn't handle non-finite values.
Results may differ from a plain program's by a relative error of at most 0.0095.
Values may be sent and summed in bfloat16 or wider, within the bound.
No kernel may reach another device: no remote copies, remote signals or barrier semaphores. Data moves between devices by JAX's collectives and lax.ppermute only.
A program may use at most 128 MiB of HBM per device.

v0:
```python
import jax
import jax.numpy as jnp
from jax import lax
from jax.sharding import PartitionSpec as P

EPSILON = 1e-05


def with_halo(cells, sides, width):
    for axis, dim in sides:
        count = lax.axis_size(axis)
        head = lax.slice_in_dim(cells, 0, width, axis=dim)
        tail = lax.slice_in_dim(cells, cells.shape[dim] - width, cells.shape[dim], axis=dim)
        cells = jnp.concatenate(
            [
                lax.ppermute(tail, axis, [(i, (i + 1) % count) for i in range(count)]),
                cells,
                lax.ppermute(head, axis, [((i + 1) % count, i) for i in range(count)]),
            ],
            axis=dim,
        )
    return cells


def layer_norm(values, gains):
    center = values - jnp.mean(values, axis=-1, keepdims=True)
    spread = jnp.mean(center * center, axis=-1, keepdims=True)
    return center * lax.rsqrt(spread + EPSILON) * gains


def finish(before, inner_sum, outer, gains):
    hidden = jax.nn.silu(inner_sum).astype(jnp.bfloat16)
    output = jnp.dot(hidden, outer, preferred_element_type=jnp.float32)
    return (before.astype(jnp.float32) + layer_norm(output, gains)).astype(jnp.bfloat16)


def extended_index(neighbours, patch_columns):
    shifted_code = neighbours + (neighbours >= 4).astype(jnp.int32)
    rows_here = lax.broadcasted_iota(jnp.int32, neighbours.shape, 0)
    cols_here = lax.broadcasted_iota(jnp.int32, neighbours.shape, 1)
    row_step = shifted_code // 3 - 1
    column_step = shifted_code % 3 - 1
    return ((rows_here + 1 + row_step) * (patch_columns + 2) + cols_here + 1 + column_step).reshape(
        -1
    )


def owner_sums(receivers, messages, coarse_count, devices):
    long_count, features = messages.shape
    capacity = (2 * long_count + devices - 1) // devices
    owners = receivers // coarse_count
    matches = (owners[:, None] == lax.iota(jnp.int32, devices)[None, :]).astype(jnp.int32)
    before = jnp.cumsum(matches, axis=0) - matches
    ranking = jnp.sum(before * matches, axis=1)
    placed = owners * capacity + ranking
    bucket = jnp.zeros((devices * capacity, features), jnp.bfloat16).at[placed].set(messages)
    labels = (
        jnp.full((devices * capacity,), coarse_count, jnp.int32)
        .at[placed]
        .set(receivers % coarse_count)
    )
    arrived, arrived_tags = (
        lax.all_to_all(
            bucket.reshape(devices, capacity, features),
            ("px", "py"),
            split_axis=0,
            concat_axis=0,
            tiled=True,
        ),
        lax.all_to_all(
            labels.astype(jnp.bfloat16).reshape(devices, capacity),
            ("px", "py"),
            split_axis=0,
            concat_axis=0,
            tiled=True,
        ),
    )
    tag_values = arrived_tags.reshape(-1).astype(jnp.int32)
    chooser = (tag_values[:, None] == lax.iota(jnp.int32, coarse_count)[None, :]).astype(
        jnp.bfloat16
    )
    return lax.dot_general(
        chooser,
        arrived.reshape(-1, features),
        (((0,), (0,)), ((), ())),
        preferred_element_type=jnp.float32,
    )


def shards(
    node_latents,
    fine_edges,
    long_edges,
    neighbours,
    coarse_slots,
    long_senders,
    long_receivers,
    edge_inner,
    edge_outer,
    edge_gain,
    node_inner,
    node_outer,
    node_gain,
):
    patch_rows, patch_columns, features = node_latents.shape
    degree = fine_edges.shape[2]
    coarse_count = coarse_slots.shape[0]
    layers = edge_inner.shape[0]
    devices = lax.axis_size("px") * lax.axis_size("py")
    patch_cells = patch_rows * patch_columns
    sender_index = extended_index(neighbours, patch_columns)
    latents = node_latents.reshape(patch_cells, features)
    fine_rows = fine_edges.reshape(patch_cells * degree, features)
    long_rows = long_edges
    for layer_index in range(layers):
        edge_part = edge_inner[layer_index, :features]
        send_part = edge_inner[layer_index, features : 2 * features]
        receive_part = edge_inner[layer_index, 2 * features :]
        own_coarse = jnp.take(latents, coarse_slots, axis=0)
        coarse = lax.all_gather(own_coarse, ("px", "py"), axis=0, tiled=True)
        padded = with_halo(
            latents.reshape(patch_rows, patch_columns, features), (("px", 0), ("py", 1)), 1
        )
        sender_terms = jnp.dot(
            padded.reshape(-1, features), send_part, preferred_element_type=jnp.float32
        )
        receiver_terms = jnp.dot(latents, receive_part, preferred_element_type=jnp.float32)
        inner_sum = jnp.dot(fine_rows, edge_part, preferred_element_type=jnp.float32) + jnp.take(
            sender_terms, sender_index, axis=0
        )
        inner_sum = (
            inner_sum.reshape(patch_cells, degree, -1) + receiver_terms[:, None, :]
        ).reshape(patch_cells * degree, -1)
        fine_rows = finish(fine_rows, inner_sum, edge_outer[layer_index], edge_gain[layer_index])
        long_sum = jnp.dot(long_rows, edge_part, preferred_element_type=jnp.float32)
        long_sum = long_sum + jnp.dot(
            jnp.take(coarse, long_senders, axis=0), send_part, preferred_element_type=jnp.float32
        )
        long_sum = long_sum + jnp.dot(
            jnp.take(coarse, long_receivers, axis=0),
            receive_part,
            preferred_element_type=jnp.float32,
        )
        long_rows = finish(long_rows, long_sum, edge_outer[layer_index], edge_gain[layer_index])
        coarse_sum = owner_sums(long_receivers, long_rows, coarse_count, devices)
        incoming = jnp.sum(
            fine_rows.reshape(patch_cells, degree, features), axis=1, dtype=jnp.float32
        )
        incoming = incoming.at[coarse_slots].add(coarse_sum).astype(jnp.bfloat16)
        node_sum = jnp.dot(
            latents, node_inner[layer_index, :features], preferred_element_type=jnp.float32
        )
        node_sum = node_sum + jnp.dot(
            incoming, node_inner[layer_index, features:], preferred_element_type=jnp.float32
        )
        latents = finish(latents, node_sum, node_outer[layer_index], node_gain[layer_index])
    return (
        latents.reshape(patch_rows, patch_columns, features),
        fine_rows.reshape(fine_edges.shape),
        long_rows,
    )


def solution(mesh):
    in_specs = (
        P("px", "py", None),
        P("px", "py", None, None),
        P(("px", "py"), None),
        P("px", "py", None),
        P(("px", "py")),
        P(("px", "py")),
        P(("px", "py")),
        P(),
        P(),
        P(),
        P(),
        P(),
        P(),
    )
    out_specs = (P("px", "py", None), P("px", "py", None, None), P(("px", "py"), None))
    return jax.shard_map(shards, mesh=mesh, in_specs=in_specs, out_specs=out_specs, check_vma=False)
```

profile of v0, /device:TPU:1, one launch (start us, length us, event | category | flops | bytes accessed | tf_op | source)
XLA Modules:
  0.0 250.8 jit_solution(7708276694184682371)
XLA Ops:
  7.3 1.8 fusion.141
  9.1 5.8 %collective-permute-start.1 = (bf16[1,20,512]{2,0,1:T(2,128)(2,1)}, bf16[1,20,512]{2,0,1:T(2,128)(2,1)S(1)}, u32[]{:S(2)}, u32[]{:S(2)}) collective-permute-start(bf16[1,20,512]{2,0,1:T(2,128)(2,1)} %get-tuple-element.22), channel_id=1, source_target_pairs={{8,0},{16,8},{24,16},{32,24},{40,32},{48,40},{56,48},{64,56},{72,6... | collective-permute-start | bytes 61448 | tf_op jit(solution)/shard_map/ppermute | solution.py:18
  22.0 10.6 %all-to-all-start = ((bf16[128,1,3]{2,1,0:T(2,128)(2,1)}), bf16[128,1,3]{2,1,0:T(2,128)(2,1)S(1)}, u32[]{:S(2)}, u32[]{:S(2)}) async-start(bf16[128,1,3]{2,1,0:T(2,128)(2,1)} %all_to_all.17), calls=%async_computation | async-start | bytes 131072 | tf_op jit(solution)/shard_map/all_to_all | solution.py:70
  37.4 2.3 fusion.33
  39.6 2.2 fusion.42
  41.9 2.7 %copy.29 = bf16[16,20,6,512]{3,2,1,0:T(8,128)(2,1)S(1)} copy(bf16[16,20,6,512]{3,0,2,1:T(8,128)(2,1)} %param.20) | data formatting | bytes 3932160 | tf_op args[1]
  44.6 2.1 reshape.173
  46.6 4.1 %add.211 = f32[320,6,512]{2,1,0:T(8,128)} broadcast(f32[320,512]{1,0:T(8,128)} %fusion.33), dimensions={0,2} | broadcast | bytes 4587520 | tf_op jit(solution)/shard_map/add | solution.py:132
  50.7 5.6 %add.212 = f32[1920,512]{1,0:T(8,128)} reshape(f32[320,6,512]{2,1,0:T(8,128)} %add.211) | data formatting | bytes 7864320 | tf_op jit(solution)/shard_map/add | solution.py:132
  58.6 1.5 collective-permute-done.3
  62.7 6.2 %gather_fusion = f32[1920,512]{1,0:T(8,128)} fusion(f32[396,512]{1,0:T(8,128)S(1)} %fusion.36, s32[2048]{0:T(1024)S(1)} %pad_clamp_fusion), kind=kCustom, calls=%fused_computation.clone | custom fusion | bytes 7872000 | tf_op jit(solution)/shard_map/jit(_take)/gather | solution.py:128
  68.9 8.3 %fusion.144 = (f32[1920]{0:T(1024)S(1)}, f32[1920,512]{1,0:T(8,128)}) fusion(bf16[2,512,512]{2,1,0:T(8,128)(2,1)} %param.27, f32[1920,512]{1,0:T(8,128)} %add.212, f32[1920,512]{1,0:T(8,128)} %gather_fusion, bf16[1920,512]{1,0:T(8,128)(2,1)S(1)} %copy-done.2, pred[1920]{0:T(1024)(128)(4,1)S(1)} %copy-done.27, bf16[2,1536,512]{2,1,0:T(8,128)(2,1)} %param.26), kind=kOutput, calls=%fused_computation.210 | convolution fusion | flops 2022111360 | bytes 14820736 | tf_op jit(solution)/shard_map/dot_general | solution.py:33
  77.2 2.8 %multiply_reduce_fusion.1 = f32[1920]{0:T(1024)S(1)} fusion(f32[1920,512]{1,0:T(8,128)} %get-tuple-element.31, f32[1920]{0:T(1024)S(1)} %broadcast_multiply_fusion.1), kind=kLoop, calls=%fused_computation.21 | loop fusion | flops 2947200 | bytes 3947520 | tf_op jit(solution)/shard_map/reduce_sum | solution.py:27
  80.0 7.5 %all-gather.5.cloned.1.call-done = bf16[128,20,512]{2,1,0:T(8,128)(2,1)} async-done(((bf16[1,20,512]{2,1,0:T(8,128)(2,1)}), bf16[128,20,512]{2,1,0:T(8,128)(2,1)}) %all-gather.5.cloned.1.call-update) | async-done | bytes 2621456 | tf_op jit(solution)/shard_map/all_gather | solution.py:120
  87.5 3.6 %reshape.308 = bf16[2560,512]{1,0:T(8,128)(2,1)S(1)} reshape(bf16[128,20,512]{2,1,0:T(8,128)(2,1)} %all-gather.5.cloned.1.call-done) | data formatting | bytes 5242880
  91.2 1.6 gather_fusion.2
  92.8 1.6 gather_fusion.3
  95.8 1.9 fusion.147
  98.1 1.4 scatter_custom_fusion.1
  100.6 5.3 %all-to-all-start.1 = ((bf16[128,3,512]{2,1,0:T(4,128)(2,1)}), bf16[128,3,512]{2,1,0:T(4,128)(2,1)S(1)}, u32[]{:S(2)}, u32[]{:S(2)}) async-start(bf16[128,3,512]{2,1,0:T(4,128)(2,1)} %reshape.178), calls=%async_computation.1 | async-start | bytes 1048576 | tf_op jit(solution)/shard_map/all_to_all | solution.py:63
  106.1 3.4 %add_convert_fusion.1 = bf16[1920,512]{1,0:T(8,128)(2,1)S(1)} fusion(bf16[1920,512]{1,0:T(8,128)(2,1)} %reshape.173, f32[1920,512]{1,0:T(8,128)} %get-tuple-element.31, f32[512]{0:T(512)S(1)} %bitcast.134, f32[1920]{0:T(1024)S(1)} %add_rsqrt_fusion.1, f32[1920]{0:T(1024)S(1)} %broadcast_multiply_fusion.1), kind=kLoop, calls=%fused_computation.20 | loop fusion | flops 5898240 | bytes 7881728 | tf_op jit(solution)/shard_map/convert_element_type | solution.py:34
  109.5 2.8 %reshape.186 = f32[320,6,512]{2,1,0:T(8,128)} reshape(bf16[1920,512]{1,0:T(8,128)(2,1)S(1)} %add_convert_fusion.1) | data formatting | bytes 5898240 | tf_op jit(solution)/shard_map/convert_element_type | solution.py:146
  112.4 5.0 %reduce_sum.141 = f32[320,512]{1,0:T(8,128)} reduce(f32[320,6,512]{2,1,0:T(8,128)} %reshape.186, f32[]{:T(128)} %constant.121.clone.1), dimensions={1}, to_apply=%region_2.4 | reduce | flops 819200 | bytes 4587524 | tf_op jit(solution)/shard_map/reduce_sum | solution.py:146
  117.3 2.1 all-to-all-done.1
  121.8 2.6 %scatter_fusion = f32[320,512]{1,0:T(8,128)} fusion(f32[320,512]{1,0:T(8,128)} %reduce_sum.141, s32[20]{0:T(128)S(1)} %copy-done.19, f32[20,512]{1,0:T(8,128)S(1)} %fusion.89), kind=kCustom, calls=%fused_computation.10 | custom fusion | flops 10240 | bytes 122960 | tf_op jit(solution)/shard_map/scatter-add | solution.py:149
  124.4 2.3 fusion.152
  128.5 2.0 fusion.20
  131.0 2.2 fusion.24
  133.3 4.5 %collective-permute-start.5 = (bf16[1,20,512]{2,1,0:T(8,128)(2,1)S(1)}, bf16[1,20,512]{2,1,0:T(8,128)(2,1)S(1)}, u32[]{:S(2)}, u32[]{:S(2)}) collective-permute-start(bf16[1,20,512]{2,1,0:T(8,128)(2,1)S(1)} %get-tuple-element.19), channel_id=1, source_target_pairs={{8,0},{16,8},{24,16},{32,24},{40,32},{48,40},{56,48},{64,56},{72,6... | collective-permute-start | bytes 61448 | tf_op jit(solution)/shard_map/ppermute | solution.py:18
  138.8 2.4 collective-permute-start.7
  142.5 3.0 %add.231 = f32[320,6,512]{2,1,0:T(8,128)} broadcast(f32[320,512]{1,0:T(8,128)S(1)} %fusion.15), dimensions={0,2} | broadcast | bytes 4587520 | tf_op jit(solution)/shard_map/add | solution.py:132
  145.5 5.5 %add.232 = f32[1920,512]{1,0:T(8,128)} reshape(f32[320,6,512]{2,1,0:T(8,128)} %add.231) | data formatting | bytes 7864320 | tf_op jit(solution)/shard_map/add | solution.py:132
  152.9 6.4 %gather_fusion.4 = f32[1920,512]{1,0:T(8,128)} fusion(f32[396,512]{1,0:T(8,128)S(1)} %fusion.18, s32[2048]{0:T(1024)} %copy-done.10), kind=kCustom, calls=%fused_computation.3.clone | custom fusion | bytes 7872000 | tf_op jit(solution)/shard_map/jit(_take)/gather | solution.py:128
  159.3 8.1 %fusion.157 = (f32[1920]{0:T(1024)S(1)}, f32[1920,512]{1,0:T(8,128)}) fusion(bf16[2,512,512]{2,1,0:T(8,128)(2,1)} %param.27, f32[1920,512]{1,0:T(8,128)} %add.232, f32[1920,512]{1,0:T(8,128)} %gather_fusion.4, pred[1920]{0:T(1024)(128)(4,1)S(1)} %copy-done.28, bf16[1920,512]{1,0:T(8,128)(2,1)S(1)} %add_convert_fusion.1, bf16[2,1536,512]{2,1,0:T(8,128)(2,1)} %param.26), kind=kOutput, calls=%fused_computation.213 | convolution fusion | flops 2022111360 | bytes 14820736 | tf_op jit(solution)/shard_map/dot_general | solution.py:33
  167.4 2.8 %multiply_reduce_fusion = f32[1920]{0:T(1024)S(1)} fusion(f32[1920,512]{1,0:T(8,128)} %get-tuple-element.37, f32[1920]{0:T(1024)S(1)} %broadcast_multiply_fusion), kind=kLoop, calls=%fused_computation.18 | loop fusion | flops 2947200 | bytes 3947520 | tf_op jit(solution)/shard_map/reduce_sum | solution.py:27
  170.3 24.0 %all-gather.7.cloned.1.call-done = bf16[128,20,512]{2,1,0:T(8,128)(2,1)} async-done(((bf16[1,20,512]{2,1,0:T(8,128)(2,1)}), bf16[128,20,512]{2,1,0:T(8,128)(2,1)}) %all-gather.7.cloned.1.call-update) | async-done | bytes 2621456 | tf_op jit(solution)/shard_map/all_gather | solution.py:120
  194.3 5.2 %reshape.310 = bf16[2560,512]{1,0:T(8,128)(2,1)} reshape(bf16[128,20,512]{2,1,0:T(8,128)(2,1)} %all-gather.7.cloned.1.call-done) | data formatting | bytes 5242880
  199.5 3.2 %gather_fusion.6 = bf16[160,512]{1,0:T(8,128)(2,1)S(1)} fusion(bf16[2560,512]{1,0:T(8,128)(2,1)} %reshape.310, s32[1024]{0:T(1024)} %copy-done.16), kind=kCustom, calls=%fused_computation.6.clone | custom fusion | bytes 328320 | tf_op jit(solution)/shard_map/jit(_take)/gather | solution.py:137
  202.7 3.2 %gather_fusion.7 = bf16[160,512]{1,0:T(8,128)(2,1)S(1)} fusion(bf16[2560,512]{1,0:T(8,128)(2,1)} %reshape.310, s32[1024]{0:T(1024)} %copy-done.15), kind=kCustom, calls=%fused_computation.7.clone | custom fusion | bytes 328320 | tf_op jit(solution)/shard_map/jit(_take)/gather | solution.py:140
  207.3 1.8 fusion.160
  212.0 5.7 %all-to-all-start.2 = ((bf16[128,3,512]{2,1,0:T(4,128)(2,1)}), bf16[128,3,512]{2,1,0:T(4,128)(2,1)}, u32[]{:S(2)}, u32[]{:S(2)}) async-start(bf16[128,3,512]{2,1,0:T(4,128)(2,1)} %reshape.182), calls=%async_computation.2 | async-start | bytes 1048576 | tf_op jit(solution)/shard_map/all_to_all | solution.py:63
  217.8 3.7 %add_convert_fusion = bf16[1920,512]{1,0:T(8,128)(2,1)} fusion(f32[1920,512]{1,0:T(8,128)} %get-tuple-element.37, f32[512]{0:T(512)S(1)} %bitcast.132, f32[1920]{0:T(1024)S(1)} %add_rsqrt_fusion, f32[1920]{0:T(1024)S(1)} %broadcast_multiply_fusion, bf16[1920,512]{1,0:T(8,128)(2,1)S(1)} %add_convert_fusion.1), kind=kLoop, calls=%fused_computation.17 | loop fusion | flops 5898240 | bytes 7881728 | tf_op jit(solution)/shard_map/convert_element_type | solution.py:34
  221.5 4.6 %reshape.189 = f32[320,6,512]{2,1,0:T(8,128)} reshape(bf16[1920,512]{1,0:T(8,128)(2,1)} %add_convert_fusion) | data formatting | bytes 5898240 | tf_op jit(solution)/shard_map/convert_element_type | solution.py:146
  226.1 2.3 reshape.185
  228.4 5.2 %reduce_sum.149 = f32[320,512]{1,0:T(8,128)} reduce(f32[320,6,512]{2,1,0:T(8,128)} %reshape.189, f32[]{:T(128)} %constant.121.clone.1), dimensions={1}, to_apply=%region_15.19 | reduce | flops 819200 | bytes 4587524 | tf_op jit(solution)/shard_map/reduce_sum | solution.py:146
  233.6 2.4 copy.36
  237.6 2.7 %scatter_fusion.1 = f32[320,512]{1,0:T(8,128)} fusion(f32[320,512]{1,0:T(8,128)} %reduce_sum.149, s32[20]{0:T(128)S(1)} %copy-done.20, f32[20,512]{1,0:T(8,128)S(1)} %fusion.88), kind=kCustom, calls=%fused_computation.12 | custom fusion | flops 10240 | bytes 122960 | tf_op jit(solution)/shard_map/scatter-add | solution.py:149
  240.3 2.4 fusion.165
  (172 shorter events, 35.8 us)
Async XLA Ops:
  7.2 26.0 %copy-start.31 = (s32[160]{0:T(256)S(1)}, s32[160]{0:T(256)}, u32[]{:S(2)}) copy-start(s32[160]{0:T(256)} %param.25) | copy-start | bytes 1924
  7.2 25.5 %copy-start.11 = (s32[16,20,6]{1,0,2:T(8,128)S(1)}, s32[16,20,6]{1,0,2:T(8,128)}, u32[]{:S(2)}) copy-start(s32[16,20,6]{1,0,2:T(8,128)} %param.22) | copy-start | bytes 23044
  7.2 26.6 %copy-start.30 = (s32[160]{0:T(256)S(1)}, s32[160]{0:T(256)}, u32[]{:S(2)}) copy-start(s32[160]{0:T(256)} %param.24) | copy-start | bytes 1924
  7.2 27.1 %copy-start.21 = (f32[2,512]{1,0:T(2,128)S(1)}, f32[2,512]{1,0:T(2,128)}, u32[]{:S(2)}) copy-start(f32[2,512]{1,0:T(2,128)} %param.28) | copy-start | bytes 12292
  7.2 27.7 %copy-start.22 = (f32[2,512]{1,0:T(2,128)S(1)}, f32[2,512]{1,0:T(2,128)}, u32[]{:S(2)}) copy-start(f32[2,512]{1,0:T(2,128)} %param.31) | copy-start | bytes 12292
  7.2 28.9 %copy-start.7 = (bf16[160,512]{1,0:T(8,128)(2,1)S(1)}, bf16[160,512]{1,0:T(8,128)(2,1)}, u32[]{:S(2)}) copy-start(bf16[160,512]{1,0:T(8,128)(2,1)} %param.21) | copy-start | bytes 491524
  7.2 80.3 %all-gather.5.cloned.1.call-start = ((), (), s32[]{:S(2)}) async-start(), calls=%async_computation.3 | async-start | bytes 3170304 | tf_op jit(solution)/shard_map/all_gather | solution.py:120
  9.1 47.2 %collective-permute-start.1 = (bf16[1,20,512]{2,0,1:T(2,128)(2,1)}, bf16[1,20,512]{2,0,1:T(2,128)(2,1)S(1)}, u32[]{:S(2)}, u32[]{:S(2)}) collective-permute-start(bf16[1,20,512]{2,0,1:T(2,128)(2,1)} %get-tuple-element.22), channel_id=1, source_target_pairs={{8,0},{16,8},{24,16},{32,24},{40,32},{48,40},{56,48},{64,56},{72,6... | collective-permute-start | bytes 61448 | tf_op jit(solution)/shard_map/ppermute | solution.py:18
  14.9 41.5 %collective-permute-start = (bf16[1,20,512]{2,0,1:T(2,128)(2,1)S(1)}, bf16[1,20,512]{2,0,1:T(2,128)(2,1)S(1)}, u32[]{:S(2)}, u32[]{:S(2)}) collective-permute-start(bf16[1,20,512]{2,0,1:T(2,128)(2,1)S(1)} %get-tuple-element.21), channel_id=1, source_target_pairs={{0,8},{8,16},{16,24},{24,32},{32,40},{40,48},{48,56},{56,64},{64,7... | collective-permute-start | bytes 61448 | tf_op jit(solution)/shard_map/ppermute | solution.py:16
  16.7 3.0 %copy-start.18 = (s32[20]{0:T(128)}, s32[20]{0:T(128)S(1)}, u32[]{:S(2)}) copy-start(s32[20]{0:T(128)S(1)} %compare_select_fusion.4) | copy-start | bytes 244
  17.4 16.9 %copy-start.25 = (pred[20]{0:T(512)(128)(4,1)}, pred[20]{0:T(512)(128)(4,1)S(1)}, u32[]{:S(2)}) copy-start(pred[20]{0:T(512)(128)(4,1)S(1)} %compare_and_fusion.3) | copy-start | bytes 64
  20.0 13.1 %copy-start.29 = (s32[160]{0:T(256)}, s32[160]{0:T(256)S(1)}, u32[]{:S(2)}) copy-start(s32[160]{0:T(256)S(1)} %compare_select_fusion.3) | copy-start | bytes 1924
  22.0 36.2 %all-to-all-start = ((bf16[128,1,3]{2,1,0:T(2,128)(2,1)}), bf16[128,1,3]{2,1,0:T(2,128)(2,1)S(1)}, u32[]{:S(2)}, u32[]{:S(2)}) async-start(bf16[128,1,3]{2,1,0:T(2,128)(2,1)} %all_to_all.17), calls=%async_computation | async-start | bytes 131072 | tf_op jit(solution)/shard_map/all_to_all | solution.py:70
  33.2 29.5 %copy-start.10 = (s32[2048]{0:T(1024)}, s32[2048]{0:T(1024)S(1)}, u32[]{:S(2)}) copy-start(s32[2048]{0:T(1024)S(1)} %pad_clamp_fusion) | copy-start | bytes 24580
  41.9 49.3 %copy-start.16 = (s32[1024]{0:T(1024)}, s32[1024]{0:T(1024)S(1)}, u32[]{:S(2)}) copy-start(s32[1024]{0:T(1024)S(1)} %get-tuple-element.43) | copy-start | bytes 12292
  41.9 50.9 %copy-start.15 = (s32[1024]{0:T(1024)}, s32[1024]{0:T(1024)S(1)}, u32[]{:S(2)}) copy-start(s32[1024]{0:T(1024)S(1)} %get-tuple-element.42) | copy-start | bytes 12292
  50.7 5.6 %copy-start.3 = (bf16[16,20,512]{2,0,1:T(8,128)(2,1)S(1)}, bf16[16,20,512]{2,0,1:T(8,128)(2,1)}, u32[]{:S(2)}) copy-start(bf16[16,20,512]{2,0,1:T(8,128)(2,1)} %param.19) | copy-start | bytes 983044
  56.4 3.7 %collective-permute-start.3 = (bf16[18,1,512]{2,0,1:T(8,128)(2,1)S(1)}, bf16[18,1,512]{2,0,1:T(8,128)(2,1)S(1)}, u32[]{:S(2)}, u32[]{:S(2)}) collective-permute-start(bf16[18,1,512]{2,0,1:T(8,128)(2,1)S(1)} %get-tuple-element.18), channel_id=1, source_target_pairs={{1,0},{2,1},{3,2},{4,3},{5,4},{6,5},{7,6},{0,7},{9,8},{10,9},{11,1... | collective-permute-start | bytes 55304 | tf_op jit(solution)/shard_map/ppermute | solution.py:18
  57.6 3.1 %collective-permute-start.2 = (bf16[18,1,512]{2,0,1:T(8,128)(2,1)S(1)}, bf16[18,1,512]{2,0,1:T(8,128)(2,1)S(1)}, u32[]{:S(2)}, u32[]{:S(2)}) collective-permute-start(bf16[18,1,512]{2,0,1:T(8,128)(2,1)S(1)} %get-tuple-element.17), channel_id=1, source_target_pairs={{0,1},{1,2},{2,3},{3,4},{4,5},{5,6},{6,7},{7,0},{8,9},{9,10},{10,1... | collective-permute-start | bytes 55304 | tf_op jit(solution)/shard_map/ppermute | solution.py:16
  58.6 61.9 %copy-start.12 = (s32[384]{0:T(512)}, s32[384]{0:T(512)S(1)}, u32[]{:S(2)}) copy-start(s32[384]{0:T(512)S(1)} %reshape.188) | copy-start | bytes 4612
  62.7 6.2 %copy-start.2 = (bf16[1920,512]{1,0:T(8,128)(2,1)S(1)}, bf16[1920,512]{1,0:T(8,128)(2,1)}, u32[]{:S(2)}) copy-start(bf16[1920,512]{1,0:T(8,128)(2,1)} %reshape.173) | copy-start | bytes 5898244
  62.7 6.2 %copy-start.27 = (pred[1920]{0:T(1024)(128)(4,1)S(1)}, pred[1920]{0:T(1024)(128)(4,1)}, u32[]{:S(2)}) copy-start(pred[1920]{0:T(1024)(128)(4,1)} %compare_and_fusion) | copy-start | bytes 5764
  80.0 14.4 %copy-start.23 = (pred[160]{0:T(512)(128)(4,1)S(1)}, pred[160]{0:T(512)(128)(4,1)}, u32[]{:S(2)}) copy-start(pred[160]{0:T(512)(128)(4,1)} %compare_and_fusion.2) | copy-start | bytes 484
  91.2 4.7 %copy-start.32 = (pred[160]{0:T(512)(128)(4,1)S(1)}, pred[160]{0:T(512)(128)(4,1)}, u32[]{:S(2)}) copy-start(pred[160]{0:T(512)(128)(4,1)} %compare_and_fusion.1) | copy-start | bytes 484
  92.8 5.2 %copy-start.8 = (bf16[160,512]{1,0:T(8,128)(2,1)S(1)}, bf16[160,512]{1,0:T(8,128)(2,1)}, u32[]{:S(2)}) copy-start(bf16[160,512]{1,0:T(8,128)(2,1)} %param.21) | copy-start | bytes 491524
  98.1 30.4 %copy-start.4 = (bf16[160,512]{1,0:T(8,128)(2,1)}, bf16[160,512]{1,0:T(8,128)(2,1)S(1)}, u32[]{:S(2)}) copy-start(bf16[160,512]{1,0:T(8,128)(2,1)S(1)} %add_convert_fusion.5) | copy-start | bytes 491524
  100.6 18.8 %all-to-all-start.1 = ((bf16[128,3,512]{2,1,0:T(4,128)(2,1)}), bf16[128,3,512]{2,1,0:T(4,128)(2,1)S(1)}, u32[]{:S(2)}, u32[]{:S(2)}) async-start(bf16[128,3,512]{2,1,0:T(4,128)(2,1)} %reshape.178), calls=%async_computation.1 | async-start | bytes 1048576 | tf_op jit(solution)/shard_map/all_to_all | solution.py:63
  105.9 88.4 %all-gather.7.cloned.1.call-start = ((), (), s32[]{:S(2)}) async-start(), calls=%async_computation.4 | async-start | bytes 3170304 | tf_op jit(solution)/shard_map/all_gather | solution.py:120
  112.4 9.4 %copy-start.19 = (s32[20]{0:T(128)S(1)}, s32[20]{0:T(128)}, u32[]{:S(2)}) copy-start(s32[20]{0:T(128)} %copy-done.18) | copy-start | bytes 244
  124.4 3.4 %copy-start.26 = (pred[20]{0:T(512)(128)(4,1)S(1)}, pred[20]{0:T(512)(128)(4,1)}, u32[]{:S(2)}) copy-start(pred[20]{0:T(512)(128)(4,1)} %copy-done.25) | copy-start | bytes 64
  130.6 7.2 %collective-permute-start.4 = (bf16[1,20,512]{2,1,0:T(8,128)(2,1)S(1)}, bf16[1,20,512]{2,1,0:T(8,128)(2,1)S(1)}, u32[]{:S(2)}, u32[]{:S(2)}) collective-permute-start(bf16[1,20,512]{2,1,0:T(8,128)(2,1)S(1)} %get-tuple-element.20), channel_id=1, source_target_pairs={{0,8},{8,16},{16,24},{24,32},{32,40},{40,48},{48,56},{56,64},{64,7... | collective-permute-start | bytes 61448 | tf_op jit(solution)/shard_map/ppermute | solution.py:16
  133.3 5.4 %collective-permute-start.5 = (bf16[1,20,512]{2,1,0:T(8,128)(2,1)S(1)}, bf16[1,20,512]{2,1,0:T(8,128)(2,1)S(1)}, u32[]{:S(2)}, u32[]{:S(2)}) collective-permute-start(bf16[1,20,512]{2,1,0:T(8,128)(2,1)S(1)} %get-tuple-element.19), channel_id=1, source_target_pairs={{8,0},{16,8},{24,16},{32,24},{40,32},{48,40},{56,48},{64,56},{72,6... | collective-permute-start | bytes 61448 | tf_op jit(solution)/shard_map/ppermute | solution.py:18
  138.8 12.3 %collective-permute-start.7 = (bf16[18,1,512]{2,1,0:T(2,128)(2,1)S(1)}, bf16[18,1,512]{2,1,0:T(2,128)(2,1)S(1)}, u32[]{:S(2)}, u32[]{:S(2)}) collective-permute-start(bf16[18,1,512]{2,1,0:T(2,128)(2,1)S(1)} %get-tuple-element.16), channel_id=1, source_target_pairs={{1,0},{2,1},{3,2},{4,3},{5,4},{6,5},{7,6},{0,7},{9,8},{10,9},{11,1... | collective-permute-start | bytes 55304 | tf_op jit(solution)/shard_map/ppermute | solution.py:18
  141.2 9.9 %collective-permute-start.6 = (bf16[18,1,512]{2,1,0:T(2,128)(2,1)S(1)}, bf16[18,1,512]{2,1,0:T(2,128)(2,1)S(1)}, u32[]{:S(2)}, u32[]{:S(2)}) collective-permute-start(bf16[18,1,512]{2,1,0:T(2,128)(2,1)S(1)} %get-tuple-element.15), channel_id=1, source_target_pairs={{0,1},{1,2},{2,3},{3,4},{4,5},{5,6},{6,7},{7,0},{8,9},{9,10},{10,1... | collective-permute-start | bytes 55304 | tf_op jit(solution)/shard_map/ppermute | solution.py:16
  152.9 6.4 %copy-start.28 = (pred[1920]{0:T(1024)(128)(4,1)S(1)}, pred[1920]{0:T(1024)(128)(4,1)}, u32[]{:S(2)}) copy-start(pred[1920]{0:T(1024)(128)(4,1)} %compare_and_fusion) | copy-start | bytes 5764
  170.2 35.7 %copy-start.6 = (f32[160,512]{1,0:T(8,128)S(1)}, f32[160,512]{1,0:T(8,128)}, u32[]{:S(2)}) copy-start(f32[160,512]{1,0:T(8,128)} %fusion.20) | copy-start | bytes 983044
  170.2 35.7 %copy-start.24 = (pred[160]{0:T(512)(128)(4,1)S(1)}, pred[160]{0:T(512)(128)(4,1)}, u32[]{:S(2)}) copy-start(pred[160]{0:T(512)(128)(4,1)} %compare_and_fusion.2) | copy-start | bytes 484
  199.5 7.8 %copy-start.33 = (pred[160]{0:T(512)(128)(4,1)S(1)}, pred[160]{0:T(512)(128)(4,1)}, u32[]{:S(2)}) copy-start(pred[160]{0:T(512)(128)(4,1)} %compare_and_fusion.1) | copy-start | bytes 484
  202.7 6.7 %copy-start.5 = (bf16[160,512]{1,0:T(8,128)(2,1)S(1)}, bf16[160,512]{1,0:T(8,128)(2,1)}, u32[]{:S(2)}) copy-start(bf16[160,512]{1,0:T(8,128)(2,1)} %copy-done.4) | copy-start | bytes 491524
  202.7 6.7 %copy-start.14 = (f32[1,512]{1,0:T(1,128)S(1)}, f32[1,512]{1,0:T(1,128)}, u32[]{:S(2)}) copy-start(f32[1,512]{1,0:T(1,128)} %get-tuple-element.25) | copy-start | bytes 6148
  209.5 12.0 %copy-start.9 = (bf16[160,512]{1,0:T(8,128)(2,1)}, bf16[160,512]{1,0:T(8,128)(2,1)S(1)}, u32[]{:S(2)}) copy-start(bf16[160,512]{1,0:T(8,128)(2,1)S(1)} %add_convert_fusion.4) | copy-start | bytes 491524
  212.0 23.9 %all-to-all-start.2 = ((bf16[128,3,512]{2,1,0:T(4,128)(2,1)}), bf16[128,3,512]{2,1,0:T(4,128)(2,1)}, u32[]{:S(2)}, u32[]{:S(2)}) async-start(bf16[128,3,512]{2,1,0:T(4,128)(2,1)} %reshape.182), calls=%async_computation.2 | async-start | bytes 1048576 | tf_op jit(solution)/shard_map/all_to_all | solution.py:63
  221.5 4.7 %copy-start = (bf16[1920,512]{1,0:T(8,128)(2,1)S(1)}, bf16[1920,512]{1,0:T(8,128)(2,1)}, u32[]{:S(2)}) copy-start(bf16[1920,512]{1,0:T(8,128)(2,1)} %add_convert_fusion) | copy-start | bytes 5898244
  228.4 5.2 %copy-start.1 = (bf16[16,20,6,512]{3,2,1,0:T(8,128)(2,1)S(1)}, bf16[16,20,6,512]{3,2,1,0:T(8,128)(2,1)}, u32[]{:S(2)}) copy-start(bf16[16,20,6,512]{3,2,1,0:T(8,128)(2,1)} %reshape.185) | copy-start | bytes 5898244
  233.6 3.8 %copy-start.13 = (s32[384]{0:T(512)S(1)}, s32[384]{0:T(512)}, u32[]{:S(2)}) copy-start(s32[384]{0:T(512)} %copy-done.12) | copy-start | bytes 4612
  233.6 4.1 %copy-start.20 = (s32[20]{0:T(128)S(1)}, s32[20]{0:T(128)}, u32[]{:S(2)}) copy-start(s32[20]{0:T(128)} %copy-done.18) | copy-start | bytes 244
  237.6 5.3 %copy-start.17 = (f32[1,512]{1,0:T(1,128)S(1)}, f32[1,512]{1,0:T(1,128)}, u32[]{:S(2)}) copy-start(f32[1,512]{1,0:T(1,128)} %get-tuple-element.23) | copy-start | bytes 6148
Sparse Core Ops, SparseCore 0:
  18.9 68.5 all-gather.4
  128.7 65.5 all-gather.6
where the time goes:
time: 253 us; the launch traced here: 251 us
  local copies, waits for them, and re-layouts  83.1 us (33%)
  matrix products  43.4 us (17%)
  starting transfers between devices  36.8 us (15%)
  waiting for transfers between devices  36.7 us (15%)
  other arithmetic  36.1 us (14%)
  between operations  14.7 us (6%)
    all_gather x2, waiting for transfers between devices, shards(): coarse = lax.all_gather(own_coarse, ('px', 'py'), axis=0, tiled=True)  31.5 us
    dot_general x6, matrix products, finish(): output = jnp.dot(hidden, outer, preferred_element_type=jnp.float32)  24.9 us
    add x4, local copies, waits for them, and re-layouts, shards(): inner_sum.reshape(patch_cells, degree, -1) + receiver_terms[:, None, :]  18.3 us
    unnamed x77, local copies, waits for them, and re-layouts  16 us
    ppermute x4, starting transfers between devices, with_halo(): lax.ppermute(head, axis, [((i + 1) % count, i) for i in range(count)])  13.8 us
    gather x2, local copies, waits for them, and re-layouts, shards(): jnp.take(sender_terms, sender_index, axis=0)  12.6 us
    all_to_all x2, starting transfers between devices, owner_sums(): lax.all_to_all(bucket.reshape(devices, capacity, features), ('px', 'py'),...  11 us
    all_to_all x1, starting transfers between devices, owner_sums(): lax.all_to_all(labels.astype(jnp.bfloat16).reshape(devices, capacity), ('...  10.6 us
  transfers between devices with their start and end apart: 13, of which 6 were waited for; matrix products, arithmetic and copies ran while one was open for 45% of the time, Pallas kernels for 0%

commit v1 on v0

--- a/solution.py
+++ b/solution.py
@@ -117,7 +117,12 @@
         send_part = edge_inner[layer_index, features : 2 * features]
         receive_part = edge_inner[layer_index, 2 * features :]
         own_coarse = jnp.take(latents, coarse_slots, axis=0)
-        coarse = lax.all_gather(own_coarse, ("px", "py"), axis=0, tiled=True)
+        coarse = jnp.concatenate(
+            lax.all_to_all(
+                jnp.stack([own_coarse] * lax.axis_size(("px", "py"))), ("px", "py"), 0, 0
+            ),
+            axis=0,
+        )
         padded = with_halo(
             latents.reshape(patch_rows, patch_columns, features), (("px", 0), ("py", 1)), 1
         )

time: 253 us -> 274 us (1.083)
  starting transfers between devices: 36.8 us -> 84.3 us
  waiting for transfers between devices: 36.7 us -> 18.9 us
  between operations: 14.7 us -> 1.38 us
  local copies, waits for them, and re-layouts: 83.1 us -> 86.6 us
    all_gather x2 -> x0, waiting for transfers between devices: 31.5 us -> none  [shards(): coarse = lax.all_gather(own_coarse, ('px', 'py'), axis=0, tiled=True)]
    all_to_all x2, starting transfers between devices: 11 us -> 42.2 us  [owner_sums(): lax.all_to_all(bucket.reshape(devices, capacity, features), ('px', 'py'),...]
    all_to_all x0 -> x2, starting transfers between devices: none -> 17.2 us  [shards(): lax.all_to_all(jnp.stack([own_coarse] * lax.axis_size(('px', 'py'))), ('p...]
    all_to_all x0 -> x2, waiting for transfers between devices: none -> 10.1 us  [shards(): lax.all_to_all(jnp.stack([own_coarse] * lax.axis_size(('px', 'py'))), ('p...]
    reshape x0 -> x2, local copies, waits for them, and re-layouts: none -> 8.81 us  [shards(): jnp.concatenate(lax.all_to_all(jnp.stack([own_coarse] * lax.axis_size(('p...]
    unnamed x77 -> x69, local copies, waits for them, and re-layouts: 16 us -> 7.21 us
    ppermute x4, waiting for transfers between devices: 2.37 us -> 8.5 us  [with_halo(): lax.ppermute(head, axis, [((i + 1) % count, i) for i in range(count)])]
    another operation x3 -> x5, local copies, waits for them, and re-layouts: 0.02 us -> 3.75 us  [the longest x2 3.73 us: shards(): jnp.stack([own_coarse] * lax.axis_size(('px', 'py')))]
  transfers between devices with their start and end apart: 13 -> 13, of which waited for: 6 -> 3; matrix products, arithmetic and copies ran while one was open for 45% -> 42% of each run, Pallas kernels for 0% -> 0%
where the time goes in v1:
time: 274 us; the launch traced here: 272 us
  local copies, waits for them, and re-layouts  86.6 us (32%)
  starting transfers between devices  84.3 us (31%)
  matrix products  43.1 us (16%)
  other arithmetic  37.6 us (14%)
  waiting for transfers between devices  18.9 us (7%)
    all_to_all x2, starting transfers between devices, owner_sums(): lax.all_to_all(bucket.reshape(devices, capacity, features), ('px', 'py'),...  42.2 us
    dot_general x6, matrix products, finish(): output = jnp.dot(hidden, outer, preferred_element_type=jnp.float32)  24.6 us
    add x4, local copies, waits for them, and re-layouts, shards(): inner_sum.reshape(patch_cells, degree, -1) + receiver_terms[:, None, :]  18.2 us
    all_to_all x2, starting transfers between devices, shards(): lax.all_to_all(jnp.stack([own_coarse] * lax.axis_size(('px', 'py'))), ('p...  17.2 us
    gather x2, local copies, waits for them, and re-layouts, shards(): jnp.take(sender_terms, sender_index, axis=0)  12.6 us
    ppermute x4, starting transfers between devices, with_halo(): lax.ppermute(head, axis, [((i + 1) % count, i) for i in range(count)])  12.2 us
    all_to_all x1, starting transfers between devices, owner_sums(): lax.all_to_all(labels.astype(jnp.bfloat16).reshape(devices, capacity), ('...  10.6 us
    reduce_sum x2, other arithmetic, shards(): jnp.sum(fine_rows.reshape(patch_cells, degree, features), axis=1, dtype=j...  10.1 us
  transfers between devices with their start and end apart: 13, of which 3 were waited for; matrix products, arithmetic and copies ran while one was open for 42% of the time, Pallas kernels for 0%

profile of v1, /device:TPU:1, one launch (start us, length us, event | category | flops | bytes accessed | tf_op | source)
XLA Modules:
  0.0 271.9 jit_solution(11541631771451357886)
XLA Ops:
  0.6 1.7 fusion.141
  2.3 5.8 %collective-permute-start.1 = (bf16[1,20,512]{2,0,1:T(2,128)(2,1)}, bf16[1,20,512]{2,0,1:T(2,128)(2,1)S(1)}, u32[]{:S(2)}, u32[]{:S(2)}) collective-permute-start(bf16[1,20,512]{2,0,1:T(2,128)(2,1)} %get-tuple-element.22), channel_id=1, source_target_pairs={{8,0},{16,8},{24,16},{32,24},{40,32},{48,40},{56,48},{64,56},{72,6... | collective-permute-start | bytes 61448 | tf_op jit(solution)/shard_map/ppermute | solution.py:18
  11.3 10.6 %all-to-all-start = ((bf16[128,1,3]{2,1,0:T(2,128)(2,1)}), bf16[128,1,3]{2,1,0:T(2,128)(2,1)S(1)}, u32[]{:S(2)}, u32[]{:S(2)}) async-start(bf16[128,1,3]{2,1,0:T(2,128)(2,1)} %all_to_all.25), calls=%async_computation | async-start | bytes 131072 | tf_op jit(solution)/shard_map/all_to_all | solution.py:70
  29.5 2.2 fusion.42
  31.8 2.2 fusion.33
  37.2 1.9 stack.4
  39.0 10.2 %all-to-all-start.1 = ((bf16[128,20,512]{2,1,0:T(8,128)(2,1)}), bf16[128,20,512]{2,1,0:T(8,128)(2,1)}, u32[]{:S(2)}, u32[]{:S(2)}) async-start(bf16[128,20,512]{2,1,0:T(8,128)(2,1)} %stack.4), calls=%async_computation.1 | async-start | bytes 6291456 | tf_op jit(solution)/shard_map/all_to_all | solution.py:121
  49.3 2.7 copy.29
  51.9 2.1 reshape.183
  54.0 4.1 %add.211 = f32[320,6,512]{2,1,0:T(8,128)} broadcast(f32[320,512]{1,0:T(8,128)} %fusion.33), dimensions={0,2} | broadcast | bytes 4587520 | tf_op jit(solution)/shard_map/add | solution.py:137
  58.1 5.6 %add.212 = f32[1920,512]{1,0:T(8,128)} reshape(f32[320,6,512]{2,1,0:T(8,128)} %add.211) | data formatting | bytes 7864320 | tf_op jit(solution)/shard_map/add | solution.py:137
  66.0 8.5 %collective-permute-done.3 = bf16[18,1,512]{2,0,1:T(8,128)(2,1)S(1)} collective-permute-done((bf16[18,1,512]{2,0,1:T(8,128)(2,1)S(1)}, bf16[18,1,512]{2,0,1:T(8,128)(2,1)S(1)}, u32[]{:S(2)}, u32[]{:S(2)}) %collective-permute-start.3) | collective-permute-done | bytes 18464 | tf_op jit(solution)/shard_map/ppermute | solution.py:18
  76.4 6.2 %gather_fusion = f32[1920,512]{1,0:T(8,128)} fusion(f32[396,512]{1,0:T(8,128)S(1)} %fusion.36, s32[2048]{0:T(1024)S(1)} %pad_clamp_fusion), kind=kCustom, calls=%fused_computation.clone | custom fusion | bytes 7872000 | tf_op jit(solution)/shard_map/jit(_take)/gather | solution.py:133
  82.6 8.1 %fusion.144 = (f32[1920]{0:T(1024)S(1)}, f32[1920,512]{1,0:T(8,128)}) fusion(bf16[2,512,512]{2,1,0:T(8,128)(2,1)} %param.27, f32[1920,512]{1,0:T(8,128)} %add.212, f32[1920,512]{1,0:T(8,128)} %gather_fusion, bf16[1920,512]{1,0:T(8,128)(2,1)S(1)} %copy-done.2, pred[1920]{0:T(1024)(128)(4,1)S(1)} %copy-done.26, bf16[2,1536,512]{2,1,0:T(8,128)(2,1)} %param.26), kind=kOutput, calls=%fused_computation.210 | convolution fusion | flops 2022111360 | bytes 14820736 | tf_op jit(solution)/shard_map/dot_general | solution.py:33
  90.7 2.8 %multiply_reduce_fusion.1 = f32[1920]{0:T(1024)S(1)} fusion(f32[1920,512]{1,0:T(8,128)} %get-tuple-element.31, f32[1920]{0:T(1024)S(1)} %broadcast_multiply_fusion.1), kind=kLoop, calls=%fused_computation.21 | loop fusion | flops 2947200 | bytes 3947520 | tf_op jit(solution)/shard_map/reduce_sum | solution.py:27
  93.5 3.6 %reshape.188 = bf16[2560,512]{1,0:T(8,128)(2,1)S(1)} reshape(bf16[128,20,512]{2,1,0:T(8,128)(2,1)} %all-to-all-done.1) | data formatting | bytes 5242880 | tf_op jit(solution)/shard_map/reshape | solution.py:120
  97.2 1.6 gather_fusion.2
  98.8 1.6 gather_fusion.3
  101.8 1.9 fusion.147
  106.6 19.3 %all-to-all-start.2 = ((bf16[128,3,512]{2,1,0:T(4,128)(2,1)}), bf16[128,3,512]{2,1,0:T(4,128)(2,1)S(1)}, u32[]{:S(2)}, u32[]{:S(2)}) async-start(bf16[128,3,512]{2,1,0:T(4,128)(2,1)} %reshape.189), calls=%async_computation.2 | async-start | bytes 1048576 | tf_op jit(solution)/shard_map/all_to_all | solution.py:63
  125.9 3.4 %add_convert_fusion.1 = bf16[1920,512]{1,0:T(8,128)(2,1)S(1)} fusion(bf16[1920,512]{1,0:T(8,128)(2,1)} %reshape.183, f32[1920,512]{1,0:T(8,128)} %get-tuple-element.31, f32[512]{0:T(512)S(1)} %bitcast.130, f32[1920]{0:T(1024)S(1)} %add_rsqrt_fusion.1, f32[1920]{0:T(1024)S(1)} %broadcast_multiply_fusion.1), kind=kLoop, calls=%fused_computation.20 | loop fusion | flops 5898240 | bytes 7881728 | tf_op jit(solution)/shard_map/convert_element_type | solution.py:34
  129.3 2.9 %reshape.198 = f32[320,6,512]{2,1,0:T(8,128)} reshape(bf16[1920,512]{1,0:T(8,128)(2,1)S(1)} %add_convert_fusion.1) | data formatting | bytes 5898240 | tf_op jit(solution)/shard_map/convert_element_type | solution.py:151
  132.1 5.0 %reduce_sum.141 = f32[320,512]{1,0:T(8,128)} reduce(f32[320,6,512]{2,1,0:T(8,128)} %reshape.198, f32[]{:T(128)} %constant.121.clone.1), dimensions={1}, to_apply=%region_2.4 | reduce | flops 819200 | bytes 4587524 | tf_op jit(solution)/shard_map/reduce_sum | solution.py:151
  137.1 2.0 fusion.20
  141.8 2.6 scatter_fusion
  144.4 2.3 fusion.152
  147.2 2.2 fusion.24
  151.2 3.8 %collective-permute-start.5 = (bf16[1,20,512]{2,1,0:T(8,128)(2,1)S(1)}, bf16[1,20,512]{2,1,0:T(8,128)(2,1)S(1)}, u32[]{:S(2)}, u32[]{:S(2)}) collective-permute-start(bf16[1,20,512]{2,1,0:T(8,128)(2,1)S(1)} %get-tuple-element.19), channel_id=1, source_target_pairs={{8,0},{16,8},{24,16},{32,24},{40,32},{48,40},{56,48},{64,56},{72,6... | collective-permute-start | bytes 61448 | tf_op jit(solution)/shard_map/ppermute | solution.py:18
  155.1 1.9 stack.5
  156.9 7.1 %all-to-all-start.3 = ((bf16[128,20,512]{2,1,0:T(8,128)(2,1)}), bf16[128,20,512]{2,1,0:T(8,128)(2,1)}, u32[]{:S(2)}, u32[]{:S(2)}) async-start(bf16[128,20,512]{2,1,0:T(8,128)(2,1)} %stack.5), calls=%async_computation.3 | async-start | bytes 6291456 | tf_op jit(solution)/shard_map/all_to_all | solution.py:121
  167.3 3.0 %add.231 = f32[320,6,512]{2,1,0:T(8,128)} broadcast(f32[320,512]{1,0:T(8,128)S(1)} %fusion.15), dimensions={0,2} | broadcast | bytes 4587520 | tf_op jit(solution)/shard_map/add | solution.py:137
  170.3 5.5 %add.232 = f32[1920,512]{1,0:T(8,128)} reshape(f32[320,6,512]{2,1,0:T(8,128)} %add.231) | data formatting | bytes 7864320 | tf_op jit(solution)/shard_map/add | solution.py:137
  177.7 6.4 %gather_fusion.4 = f32[1920,512]{1,0:T(8,128)} fusion(f32[396,512]{1,0:T(8,128)S(1)} %fusion.18, s32[2048]{0:T(1024)} %copy-done.10), kind=kCustom, calls=%fused_computation.3.clone | custom fusion | bytes 7872000 | tf_op jit(solution)/shard_map/jit(_take)/gather | solution.py:133
  184.1 8.1 %fusion.157 = (f32[1920]{0:T(1024)S(1)}, f32[1920,512]{1,0:T(8,128)}) fusion(bf16[2,512,512]{2,1,0:T(8,128)(2,1)} %param.27, f32[1920,512]{1,0:T(8,128)} %add.232, f32[1920,512]{1,0:T(8,128)} %gather_fusion.4, pred[1920]{0:T(1024)(128)(4,1)S(1)} %copy-done.27, bf16[1920,512]{1,0:T(8,128)(2,1)S(1)} %add_convert_fusion.1, bf16[2,1536,512]{2,1,0:T(8,128)(2,1)} %param.26), kind=kOutput, calls=%fused_computation.213 | convolution fusion | flops 2022111360 | bytes 14820736 | tf_op jit(solution)/shard_map/dot_general | solution.py:33
  192.2 2.8 %multiply_reduce_fusion = f32[1920]{0:T(1024)S(1)} fusion(f32[1920,512]{1,0:T(8,128)} %get-tuple-element.37, f32[1920]{0:T(1024)S(1)} %broadcast_multiply_fusion), kind=kLoop, calls=%fused_computation.18 | loop fusion | flops 2947200 | bytes 3947520 | tf_op jit(solution)/shard_map/reduce_sum | solution.py:27
  195.1 10.1 %all-to-all-done.3 = bf16[128,20,512]{2,1,0:T(8,128)(2,1)} async-done(((bf16[128,20,512]{2,1,0:T(8,128)(2,1)}), bf16[128,20,512]{2,1,0:T(8,128)(2,1)}, u32[]{:S(2)}, u32[]{:S(2)}) %all-to-all-start.3) | async-done | bytes 2621472 | tf_op jit(solution)/shard_map/all_to_all | solution.py:121
  205.1 5.2 %reshape.193 = bf16[2560,512]{1,0:T(8,128)(2,1)} reshape(bf16[128,20,512]{2,1,0:T(8,128)(2,1)} %all-to-all-done.3) | data formatting | bytes 5242880 | tf_op jit(solution)/shard_map/reshape | solution.py:120
  210.3 3.2 %gather_fusion.6 = bf16[160,512]{1,0:T(8,128)(2,1)S(1)} fusion(bf16[2560,512]{1,0:T(8,128)(2,1)} %reshape.193, s32[1024]{0:T(1024)} %copy-done.15), kind=kCustom, calls=%fused_computation.6.clone | custom fusion | bytes 328320 | tf_op jit(solution)/shard_map/jit(_take)/gather | solution.py:142
  213.5 3.2 %gather_fusion.7 = bf16[160,512]{1,0:T(8,128)(2,1)S(1)} fusion(bf16[2560,512]{1,0:T(8,128)(2,1)} %reshape.193, s32[1024]{0:T(1024)} %copy-done.14), kind=kCustom, calls=%fused_computation.7.clone | custom fusion | bytes 328320 | tf_op jit(solution)/shard_map/jit(_take)/gather | solution.py:145
  218.1 1.8 fusion.160
  222.8 22.9 %all-to-all-start.4 = ((bf16[128,3,512]{2,1,0:T(4,128)(2,1)}), bf16[128,3,512]{2,1,0:T(4,128)(2,1)}, u32[]{:S(2)}, u32[]{:S(2)}) async-start(bf16[128,3,512]{2,1,0:T(4,128)(2,1)} %reshape.194), calls=%async_computation.4 | async-start | bytes 1048576 | tf_op jit(solution)/shard_map/all_to_all | solution.py:63
  245.7 3.7 %add_convert_fusion = bf16[1920,512]{1,0:T(8,128)(2,1)} fusion(f32[1920,512]{1,0:T(8,128)} %get-tuple-element.37, f32[512]{0:T(512)S(1)} %bitcast.128, f32[1920]{0:T(1024)S(1)} %add_rsqrt_fusion, f32[1920]{0:T(1024)S(1)} %broadcast_multiply_fusion, bf16[1920,512]{1,0:T(8,128)(2,1)S(1)} %add_convert_fusion.1), kind=kLoop, calls=%fused_computation.17 | loop fusion | flops 5898240 | bytes 7881728 | tf_op jit(solution)/shard_map/convert_element_type | solution.py:34
  249.4 4.6 %reshape.201 = f32[320,6,512]{2,1,0:T(8,128)} reshape(bf16[1920,512]{1,0:T(8,128)(2,1)} %add_convert_fusion) | data formatting | bytes 5898240 | tf_op jit(solution)/shard_map/convert_element_type | solution.py:151
  254.1 2.3 reshape.197
  256.3 5.1 %reduce_sum.149 = f32[320,512]{1,0:T(8,128)} reduce(f32[320,6,512]{2,1,0:T(8,128)} %reshape.201, f32[]{:T(128)} %constant.121.clone.1), dimensions={1}, to_apply=%region_15.19 | reduce | flops 819200 | bytes 4587524 | tf_op jit(solution)/shard_map/reduce_sum | solution.py:151
  261.5 2.4 copy.36
  265.6 2.6 scatter_fusion.1
  268.2 2.3 fusion.165
  (166 shorter events, 39.6 us)
Async XLA Ops:
  2.3 61.4 %collective-permute-start.1 = (bf16[1,20,512]{2,0,1:T(2,128)(2,1)}, bf16[1,20,512]{2,0,1:T(2,128)(2,1)S(1)}, u32[]{:S(2)}, u32[]{:S(2)}) collective-permute-start(bf16[1,20,512]{2,0,1:T(2,128)(2,1)} %get-tuple-element.22), channel_id=1, source_target_pairs={{8,0},{16,8},{24,16},{32,24},{40,32},{48,40},{56,48},{64,56},{72,6... | collective-permute-start | bytes 61448 | tf_op jit(solution)/shard_map/ppermute | solution.py:18
  8.1 55.6 %collective-permute-start = (bf16[1,20,512]{2,0,1:T(2,128)(2,1)S(1)}, bf16[1,20,512]{2,0,1:T(2,128)(2,1)S(1)}, u32[]{:S(2)}, u32[]{:S(2)}) collective-permute-start(bf16[1,20,512]{2,0,1:T(2,128)(2,1)S(1)} %get-tuple-element.21), channel_id=1, source_target_pairs={{0,8},{8,16},{16,24},{24,32},{32,40},{40,48},{48,56},{56,64},{64,7... | collective-permute-start | bytes 61448 | tf_op jit(solution)/shard_map/ppermute | solution.py:16
  8.9 25.1 %copy-start.20 = (f32[2,512]{1,0:T(2,128)S(1)}, f32[2,512]{1,0:T(2,128)}, u32[]{:S(2)}) copy-start(f32[2,512]{1,0:T(2,128)} %param.28) | copy-start | bytes 12292
  8.9 25.7 %copy-start.7 = (bf16[160,512]{1,0:T(8,128)(2,1)S(1)}, bf16[160,512]{1,0:T(8,128)(2,1)}, u32[]{:S(2)}) copy-start(bf16[160,512]{1,0:T(8,128)(2,1)} %param.21) | copy-start | bytes 491524
  9.3 15.1 %copy-start.28 = (s32[160]{0:T(256)}, s32[160]{0:T(256)S(1)}, u32[]{:S(2)}) copy-start(s32[160]{0:T(256)S(1)} %compare_select_fusion.3) | copy-start | bytes 1924
  11.3 25.8 %all-to-all-start = ((bf16[128,1,3]{2,1,0:T(2,128)(2,1)}), bf16[128,1,3]{2,1,0:T(2,128)(2,1)S(1)}, u32[]{:S(2)}, u32[]{:S(2)}) async-start(bf16[128,1,3]{2,1,0:T(2,128)(2,1)} %all_to_all.25), calls=%async_computation | async-start | bytes 131072 | tf_op jit(solution)/shard_map/all_to_all | solution.py:70
  22.0 14.5 %copy-start.21 = (f32[2,512]{1,0:T(2,128)S(1)}, f32[2,512]{1,0:T(2,128)}, u32[]{:S(2)}) copy-start(f32[2,512]{1,0:T(2,128)} %param.31) | copy-start | bytes 12292
  25.7 11.4 %copy-start.17 = (s32[20]{0:T(128)}, s32[20]{0:T(128)S(1)}, u32[]{:S(2)}) copy-start(s32[20]{0:T(128)S(1)} %compare_select_fusion.4) | copy-start | bytes 244
  26.3 12.7 %copy-start.24 = (pred[20]{0:T(512)(128)(4,1)}, pred[20]{0:T(512)(128)(4,1)S(1)}, u32[]{:S(2)}) copy-start(pred[20]{0:T(512)(128)(4,1)S(1)} %compare_and_fusion.3) | copy-start | bytes 64
  37.2 39.2 %copy-start.10 = (s32[2048]{0:T(1024)}, s32[2048]{0:T(1024)S(1)}, u32[]{:S(2)}) copy-start(s32[2048]{0:T(1024)S(1)} %pad_clamp_fusion) | copy-start | bytes 24580
  39.0 54.5 %all-to-all-start.1 = ((bf16[128,20,512]{2,1,0:T(8,128)(2,1)}), bf16[128,20,512]{2,1,0:T(8,128)(2,1)}, u32[]{:S(2)}, u32[]{:S(2)}) async-start(bf16[128,20,512]{2,1,0:T(8,128)(2,1)} %stack.4), calls=%async_computation.1 | async-start | bytes 6291456 | tf_op jit(solution)/shard_map/all_to_all | solution.py:121
  49.2 48.0 %copy-start.15 = (s32[1024]{0:T(1024)}, s32[1024]{0:T(1024)S(1)}, u32[]{:S(2)}) copy-start(s32[1024]{0:T(1024)S(1)} %get-tuple-element.43) | copy-start | bytes 12292
  49.2 49.5 %copy-start.14 = (s32[1024]{0:T(1024)}, s32[1024]{0:T(1024)S(1)}, u32[]{:S(2)}) copy-start(s32[1024]{0:T(1024)S(1)} %get-tuple-element.42) | copy-start | bytes 12292
  58.1 5.6 %copy-start.3 = (bf16[16,20,512]{2,0,1:T(8,128)(2,1)S(1)}, bf16[16,20,512]{2,0,1:T(8,128)(2,1)}, u32[]{:S(2)}) copy-start(bf16[16,20,512]{2,0,1:T(8,128)(2,1)} %param.19) | copy-start | bytes 983044
  63.7 10.7 %collective-permute-start.3 = (bf16[18,1,512]{2,0,1:T(8,128)(2,1)S(1)}, bf16[18,1,512]{2,0,1:T(8,128)(2,1)S(1)}, u32[]{:S(2)}, u32[]{:S(2)}) collective-permute-start(bf16[18,1,512]{2,0,1:T(8,128)(2,1)S(1)} %get-tuple-element.18), channel_id=1, source_target_pairs={{1,0},{2,1},{3,2},{4,3},{5,4},{6,5},{7,6},{0,7},{9,8},{10,9},{11,1... | collective-permute-start | bytes 55304 | tf_op jit(solution)/shard_map/ppermute | solution.py:18
  65.1 9.4 %collective-permute-start.2 = (bf16[18,1,512]{2,0,1:T(8,128)(2,1)S(1)}, bf16[18,1,512]{2,0,1:T(8,128)(2,1)S(1)}, u32[]{:S(2)}, u32[]{:S(2)}) collective-permute-start(bf16[18,1,512]{2,0,1:T(8,128)(2,1)S(1)} %get-tuple-element.17), channel_id=1, source_target_pairs={{0,1},{1,2},{2,3},{3,4},{4,5},{5,6},{6,7},{7,0},{8,9},{9,10},{10,1... | collective-permute-start | bytes 55304 | tf_op jit(solution)/shard_map/ppermute | solution.py:16
  66.0 74.6 %copy-start.11 = (s32[384]{0:T(512)}, s32[384]{0:T(512)S(1)}, u32[]{:S(2)}) copy-start(s32[384]{0:T(512)S(1)} %reshape.200) | copy-start | bytes 4612
  76.4 6.2 %copy-start.2 = (bf16[1920,512]{1,0:T(8,128)(2,1)S(1)}, bf16[1920,512]{1,0:T(8,128)(2,1)}, u32[]{:S(2)}) copy-start(bf16[1920,512]{1,0:T(8,128)(2,1)} %reshape.183) | copy-start | bytes 5898244
  76.4 6.2 %copy-start.26 = (pred[1920]{0:T(1024)(128)(4,1)S(1)}, pred[1920]{0:T(1024)(128)(4,1)}, u32[]{:S(2)}) copy-start(pred[1920]{0:T(1024)(128)(4,1)} %compare_and_fusion) | copy-start | bytes 5764
  93.5 6.9 %copy-start.22 = (pred[160]{0:T(512)(128)(4,1)S(1)}, pred[160]{0:T(512)(128)(4,1)}, u32[]{:S(2)}) copy-start(pred[160]{0:T(512)(128)(4,1)} %compare_and_fusion.2) | copy-start | bytes 484
  97.2 4.7 %copy-start.29 = (pred[160]{0:T(512)(128)(4,1)S(1)}, pred[160]{0:T(512)(128)(4,1)}, u32[]{:S(2)}) copy-start(pred[160]{0:T(512)(128)(4,1)} %compare_and_fusion.1) | copy-start | bytes 484
  98.8 5.2 %copy-start.8 = (bf16[160,512]{1,0:T(8,128)(2,1)S(1)}, bf16[160,512]{1,0:T(8,128)(2,1)}, u32[]{:S(2)}) copy-start(bf16[160,512]{1,0:T(8,128)(2,1)} %param.21) | copy-start | bytes 491524
  104.1 33.0 %copy-start.4 = (bf16[160,512]{1,0:T(8,128)(2,1)}, bf16[160,512]{1,0:T(8,128)(2,1)S(1)}, u32[]{:S(2)}) copy-start(bf16[160,512]{1,0:T(8,128)(2,1)S(1)} %add_convert_fusion.5) | copy-start | bytes 491524
  106.6 32.9 %all-to-all-start.2 = ((bf16[128,3,512]{2,1,0:T(4,128)(2,1)}), bf16[128,3,512]{2,1,0:T(4,128)(2,1)S(1)}, u32[]{:S(2)}, u32[]{:S(2)}) async-start(bf16[128,3,512]{2,1,0:T(4,128)(2,1)} %reshape.189), calls=%async_computation.2 | async-start | bytes 1048576 | tf_op jit(solution)/shard_map/all_to_all | solution.py:63
  132.1 9.7 %copy-start.18 = (s32[20]{0:T(128)S(1)}, s32[20]{0:T(128)}, u32[]{:S(2)}) copy-start(s32[20]{0:T(128)} %copy-done.17) | copy-start | bytes 244
  146.7 8.3 %copy-start.25 = (pred[20]{0:T(512)(128)(4,1)S(1)}, pred[20]{0:T(512)(128)(4,1)}, u32[]{:S(2)}) copy-start(pred[20]{0:T(512)(128)(4,1)} %copy-done.24) | copy-start | bytes 64
  150.1 13.9 %collective-permute-start.4 = (bf16[1,20,512]{2,1,0:T(8,128)(2,1)S(1)}, bf16[1,20,512]{2,1,0:T(8,128)(2,1)S(1)}, u32[]{:S(2)}, u32[]{:S(2)}) collective-permute-start(bf16[1,20,512]{2,1,0:T(8,128)(2,1)S(1)} %get-tuple-element.20), channel_id=1, source_target_pairs={{0,8},{8,16},{16,24},{24,32},{32,40},{40,48},{48,56},{56,64},{64,7... | collective-permute-start | bytes 61448 | tf_op jit(solution)/shard_map/ppermute | solution.py:16
  151.2 12.8 %collective-permute-start.5 = (bf16[1,20,512]{2,1,0:T(8,128)(2,1)S(1)}, bf16[1,20,512]{2,1,0:T(8,128)(2,1)S(1)}, u32[]{:S(2)}, u32[]{:S(2)}) collective-permute-start(bf16[1,20,512]{2,1,0:T(8,128)(2,1)S(1)} %get-tuple-element.19), channel_id=1, source_target_pairs={{8,0},{16,8},{24,16},{32,24},{40,32},{48,40},{56,48},{64,56},{72,6... | collective-permute-start | bytes 61448 | tf_op jit(solution)/shard_map/ppermute | solution.py:18
  156.9 48.2 %all-to-all-start.3 = ((bf16[128,20,512]{2,1,0:T(8,128)(2,1)}), bf16[128,20,512]{2,1,0:T(8,128)(2,1)}, u32[]{:S(2)}, u32[]{:S(2)}) async-start(bf16[128,20,512]{2,1,0:T(8,128)(2,1)} %stack.5), calls=%async_computation.3 | async-start | bytes 6291456 | tf_op jit(solution)/shard_map/all_to_all | solution.py:121
  164.2 11.7 %collective-permute-start.7 = (bf16[18,1,512]{2,1,0:T(2,128)(2,1)S(1)}, bf16[18,1,512]{2,1,0:T(2,128)(2,1)S(1)}, u32[]{:S(2)}, u32[]{:S(2)}) collective-permute-start(bf16[18,1,512]{2,1,0:T(2,128)(2,1)S(1)} %get-tuple-element.16), channel_id=1, source_target_pairs={{1,0},{2,1},{3,2},{4,3},{5,4},{6,5},{7,6},{0,7},{9,8},{10,9},{11,1... | collective-permute-start | bytes 55304 | tf_op jit(solution)/shard_map/ppermute | solution.py:18
  165.6 10.3 %collective-permute-start.6 = (bf16[18,1,512]{2,1,0:T(2,128)(2,1)S(1)}, bf16[18,1,512]{2,1,0:T(2,128)(2,1)S(1)}, u32[]{:S(2)}, u32[]{:S(2)}) collective-permute-start(bf16[18,1,512]{2,1,0:T(2,128)(2,1)S(1)} %get-tuple-element.15), channel_id=1, source_target_pairs={{0,1},{1,2},{2,3},{3,4},{4,5},{5,6},{6,7},{7,0},{8,9},{9,10},{10,1... | collective-permute-start | bytes 55304 | tf_op jit(solution)/shard_map/ppermute | solution.py:16
  177.7 6.4 %copy-start.27 = (pred[1920]{0:T(1024)(128)(4,1)S(1)}, pred[1920]{0:T(1024)(128)(4,1)}, u32[]{:S(2)}) copy-start(pred[1920]{0:T(1024)(128)(4,1)} %compare_and_fusion) | copy-start | bytes 5764
  195.0 21.7 %copy-start.6 = (f32[160,512]{1,0:T(8,128)S(1)}, f32[160,512]{1,0:T(8,128)}, u32[]{:S(2)}) copy-start(f32[160,512]{1,0:T(8,128)} %fusion.20) | copy-start | bytes 983044
  195.1 21.7 %copy-start.23 = (pred[160]{0:T(512)(128)(4,1)S(1)}, pred[160]{0:T(512)(128)(4,1)}, u32[]{:S(2)}) copy-start(pred[160]{0:T(512)(128)(4,1)} %compare_and_fusion.2) | copy-start | bytes 484
  210.3 7.8 %copy-start.30 = (pred[160]{0:T(512)(128)(4,1)S(1)}, pred[160]{0:T(512)(128)(4,1)}, u32[]{:S(2)}) copy-start(pred[160]{0:T(512)(128)(4,1)} %compare_and_fusion.1) | copy-start | bytes 484
  213.5 6.7 %copy-start.5 = (bf16[160,512]{1,0:T(8,128)(2,1)S(1)}, bf16[160,512]{1,0:T(8,128)(2,1)}, u32[]{:S(2)}) copy-start(bf16[160,512]{1,0:T(8,128)(2,1)} %copy-done.4) | copy-start | bytes 491524
  213.5 6.7 %copy-start.13 = (f32[1,512]{1,0:T(1,128)S(1)}, f32[1,512]{1,0:T(1,128)}, u32[]{:S(2)}) copy-start(f32[1,512]{1,0:T(1,128)} %get-tuple-element.25) | copy-start | bytes 6148
  220.3 29.1 %copy-start.9 = (bf16[160,512]{1,0:T(8,128)(2,1)}, bf16[160,512]{1,0:T(8,128)(2,1)S(1)}, u32[]{:S(2)}) copy-start(bf16[160,512]{1,0:T(8,128)(2,1)S(1)} %add_convert_fusion.4) | copy-start | bytes 491524
  222.8 41.0 %all-to-all-start.4 = ((bf16[128,3,512]{2,1,0:T(4,128)(2,1)}), bf16[128,3,512]{2,1,0:T(4,128)(2,1)}, u32[]{:S(2)}, u32[]{:S(2)}) async-start(bf16[128,3,512]{2,1,0:T(4,128)(2,1)} %reshape.194), calls=%async_computation.4 | async-start | bytes 1048576 | tf_op jit(solution)/shard_map/all_to_all | solution.py:63
  249.4 4.7 %copy-start = (bf16[1920,512]{1,0:T(8,128)(2,1)S(1)}, bf16[1920,512]{1,0:T(8,128)(2,1)}, u32[]{:S(2)}) copy-start(bf16[1920,512]{1,0:T(8,128)(2,1)} %add_convert_fusion) | copy-start | bytes 5898244
  256.3 5.2 %copy-start.1 = (bf16[16,20,6,512]{3,2,1,0:T(8,128)(2,1)S(1)}, bf16[16,20,6,512]{3,2,1,0:T(8,128)(2,1)}, u32[]{:S(2)}) copy-start(bf16[16,20,6,512]{3,2,1,0:T(8,128)(2,1)} %reshape.197) | copy-start | bytes 5898244
  261.5 3.8 %copy-start.12 = (s32[384]{0:T(512)S(1)}, s32[384]{0:T(512)}, u32[]{:S(2)}) copy-start(s32[384]{0:T(512)} %copy-done.11) | copy-start | bytes 4612
  261.5 4.1 %copy-start.19 = (s32[20]{0:T(128)S(1)}, s32[20]{0:T(128)}, u32[]{:S(2)}) copy-start(s32[20]{0:T(128)} %copy-done.17) | copy-start | bytes 244
  265.5 5.2 %copy-start.16 = (f32[1,512]{1,0:T(1,128)S(1)}, f32[1,512]{1,0:T(1,128)}, u32[]{:S(2)}) copy-start(f32[1,512]{1,0:T(1,128)} %get-tuple-element.23) | copy-start | bytes 6148
